TPU v7x, 512 devices: a whole 4x4x16 slice. The times are simulated.
512 devices in a mesh: pop: 16 (over z), tp: 32 (over y, x, core).
Axes of the slice: x: 4, y: 4, z: 16, core: 2. Of those that a mesh axis runs over, the one named last changes fastest.
Arguments:
- in_spikes: int32 [4, 15, 4096], replicated, may hold values 0 or 1
- w_in: bfloat16 [4096, 4096], P(None, 'tp'), may hold values from -0.1875 to 0.1875
- w_rec: bfloat16 [4096, 4096], P(None, 'tp'), may hold values from -0.1875 to 0.1875
- leak_rate: float32 [4096], P('tp'), may hold values from 0.5 to 0.95
- neuron_bias: float32 [4096], P('tp'), may hold values from -2.5 to 2.5
- readout: float32 [4096], P('tp'), may hold values from -0.1875 to 0.1875
- pert_table: bfloat16 [256, 4096], P(None, 'tp'), may hold values from -4 to 4
- pert_idx: int32 [512, 2], P('pop'), may hold values from 0 to 255
- member_ranks: int32 [512], P('pop'), may hold values from 0 to 511, each once
Outputs:
- returns: float32 [512], P('pop')
- grad_rec: bfloat16 [4096, 4096], P(None, 'tp')
Inputs may be any that keep to these rules, and one draw needn't show every extreme that they name: member_ranks holds each of 0 to 511 once.
All inputs are finite; a program needn't handle non-finite values.
Results may differ from a plain program's by a relative error of at most 0.0044.
Values may be sent and summed in bfloat16 or wider, within the bound.
A program may use at most 64 MiB of HBM per device.

v0:
```python
import jax
import jax.numpy as jnp
from jax import lax
from jax.sharding import PartitionSpec as P

sigma_scale = 0.01


def shards(
    in_spikes, w_in, w_rec, leak_rate, neuron_bias, readout, pert_table, pert_idx, member_ranks
):
    step_count, episodes, inputs = in_spikes.shape
    members_dev = pert_idx.shape[0]
    local_width = w_rec.shape[1]
    row_count = members_dev * episodes
    member_count = members_dev * lax.axis_size("pop")
    spike_input = in_spikes.astype(jnp.bfloat16).reshape(step_count * episodes, inputs)
    input_drive = jnp.dot(spike_input, w_in, preferred_element_type=jnp.float32) + neuron_bias
    input_drive = input_drive.reshape(step_count, episodes, local_width)
    post_side = jnp.take(pert_table, pert_idx[:, 1], axis=0).astype(jnp.float32)
    pre_local = jnp.take(pert_table, pert_idx[:, 0], axis=0)
    membrane = jnp.zeros((members_dev, episodes, local_width), jnp.float32)
    spikes = jnp.zeros((members_dev, episodes, local_width), jnp.bfloat16)
    readout_sum = jnp.zeros((members_dev, episodes), jnp.float32)
    for moment in range(step_count):
        current = input_drive[moment][None]
        if moment > 0:
            flat_spikes = spikes.reshape(row_count, local_width)
            recurrent = jnp.dot(
                lax.all_gather(flat_spikes, "tp", axis=1, tiled=True),
                w_rec,
                preferred_element_type=jnp.float32,
            )
            partial_proj = jnp.einsum(
                "men,mn->me", spikes, pre_local, preferred_element_type=jnp.float32
            )
            projection = lax.psum(partial_proj, "tp")
            current = (
                current
                + recurrent.reshape(members_dev, episodes, local_width)
                + sigma_scale * projection[:, :, None] * post_side[:, None, :]
            )
        membrane = leak_rate * (membrane - spikes.astype(jnp.float32)) + current
        spikes = jax.nn.sigmoid(4.0 * (membrane - 1.0)).astype(jnp.bfloat16)
        readout_sum = readout_sum + jnp.einsum(
            "men,n->me", spikes.astype(jnp.float32), readout, precision=lax.Precision.HIGHEST
        )
    returns = lax.psum(jnp.sum(readout_sum, axis=1), "tp") / (episodes * step_count)
    fitness = member_ranks.astype(jnp.float32) / (member_count - 1) - 0.5 + returns
    full_table = lax.all_gather(pert_table, "tp", axis=1, tiled=True)
    pre_side = jnp.take(full_table, pert_idx[:, 0], axis=0)
    weighted = pre_side.astype(jnp.float32) * fitness[:, None]
    partial_grad = jnp.dot(weighted.T, post_side, precision=lax.Precision.HIGHEST)
    grad_total = lax.psum(partial_grad, "pop")
    grad_rec = (grad_total * jnp.sqrt(12.0 / member_count)).astype(jnp.bfloat16)
    return (returns, grad_rec)


def solution(mesh):
    placed = (
        P(),
        P(None, "tp"),
        P(None, "tp"),
        P("tp"),
        P("tp"),
        P("tp"),
        P(None, "tp"),
        P("pop", None),
        P("pop"),
    )
    return jax.shard_map(
        shards, mesh=mesh, in_specs=placed, out_specs=(P("pop"), P(None, "tp")), check_vma=False
    )
```

profile of v0, /device:TPU:2, one launch (start us, length us, event | category | flops | bytes accessed | tf_op | source)
XLA Modules:
  0.0 627.7 jit_solution(11795909745084561978)
XLA Ops:
  7.3 1.5 convert_element_type.59
  8.7 0.3 copy.12
  9.0 0.2 reshape.59
  9.2 1.5 convolution_add_fusion
  10.8 0.7 divide_convert_fusion.5
  11.7 0.6 gather_fusion.2
  12.4 0.6 gather_fusion.1
  13.1 0.2 fusion.23
  13.3 124.6 %psum.35 = f32[32,15]{1,0:T(8,128)S(1)} all-reduce(f32[32,15]{1,0:T(8,128)S(1)} %bitcast.55), channel_id=1, replica_groups=mesh['pop'=16,'tp'=32] {'tp'}, use_global_device_ids=true, to_apply=%region_0.0 | all-reduce | flops 480 | bytes 3840 | tf_op jit(solution)/shard_map/psum | solution.py:37
  138.1 4.0 divide_convert_fusion.4
  142.2 0.7 all-gather.11.cloned.1.call-update
  143.0 0.2 divide_convert_fusion.2
  143.2 0.2 fusion.27
  143.3 124.4 %psum.36 = f32[32,15]{1,0:T(8,128)S(1)} all-reduce(f32[32,15]{1,0:T(8,128)S(1)} %bitcast.56), channel_id=1, replica_groups=mesh['pop'=16,'tp'=32] {'tp'}, use_global_device_ids=true, to_apply=%region_1.3 | all-reduce | flops 480 | bytes 3840 | tf_op jit(solution)/shard_map/psum | solution.py:37
  267.9 4.0 divide_convert_fusion.3
  272.0 2.8 gather_fusion
  274.8 0.2 fusion.19
  275.1 0.2 copy.18
  275.3 0.3 divide_convert_fusion.1
  275.6 0.2 fusion.17
  276.0 0.2 fusion.21
  276.2 0.2 copy.14
  276.4 0.2 fusion.25
  276.6 124.1 %psum.37 = f32[32,15]{1,0:T(8,128)S(1)} all-reduce(f32[32,15]{1,0:T(8,128)S(1)} %bitcast.54), channel_id=1, replica_groups=mesh['pop'=16,'tp'=32] {'tp'}, use_global_device_ids=true, to_apply=%region_2.4 | all-reduce | flops 480 | bytes 3840 | tf_op jit(solution)/shard_map/psum | solution.py:37
  400.7 3.3 fusion.42
  404.0 0.2 divide_convert_fusion
  404.2 0.2 fusion.15
  404.6 62.7 %psum.38 = f32[32]{0:T(128)S(1)} all-reduce(f32[32]{0:T(128)S(1)} %fusion.30), channel_id=1, replica_groups=mesh['pop'=16,'tp'=32] {'tp'}, use_global_device_ids=true, to_apply=%region_4.6 | all-reduce | flops 32 | bytes 256 | tf_op jit(solution)/shard_map/psum | solution.py:48
  467.3 0.5 add_add_fusion.3
  467.8 3.2 fusion
  471.0 147.4 %all-reduce.2.cloned.1.call-done = f32[4096,128]{1,0:T(8,128)} async-done(((f32[4096,128]{1,0:T(8,128)}), f32[4096,128]{1,0:T(8,128)}) %all-reduce.2.cloned.1.call-update) | async-done | bytes 2097168 | tf_op jit(solution)/shard_map/psum | solution.py:54
  618.5 2.7 multiply_convert_fusion
  (54 shorter events, 1.4 us)
Async XLA Ops:
  7.2 130.9 %copy-start = (bf16[4096,128]{1,0:T(8,128)(2,1)S(1)}, bf16[4096,128]{1,0:T(8,128)(2,1)}, u32[]{:S(2)}) copy-start(bf16[4096,128]{1,0:T(8,128)(2,1)} %param.13) | copy-start | bytes 3145732
  7.2 3.6 copy-start.3
  7.2 4.4 copy-start.4
  7.2 4.5 copy-start.1
  7.2 130.9 %all-gather.5.cloned.1.call-start = ((), (), s32[]{:S(2)}) async-start(), calls=%async_computation | async-start | bytes 4055040 | tf_op jit(solution)/shard_map/all_gather | solution.py:30
  11.6 256.3 %all-gather.7.cloned.1.call-start = ((), (), s32[]{:S(2)}) async-start(), calls=%async_computation.1 | async-start | bytes 4055040 | tf_op jit(solution)/shard_map/all_gather | solution.py:30
  142.1 129.9 %all-gather.11.cloned.1.call-start = ((), (), s32[]{:S(2)}) async-start(), calls=%async_computation.3 | async-start | bytes 2162688 | tf_op jit(solution)/shard_map/all_gather | solution.py:50
  142.8 257.8 %all-gather.9.cloned.1.call-start = ((), (), s32[]{:S(2)}) async-start(), calls=%async_computation.2 | async-start | bytes 4055040 | tf_op jit(solution)/shard_map/all_gather | solution.py:30
  267.9 7.0 %copy-start.2 = (f32[128]{0:T(128)S(1)}, f32[128]{0:T(128)}, u32[]{:S(2)}) copy-start(f32[128]{0:T(128)} %param.16) | copy-start | bytes 1540
  271.9 346.6 %all-reduce.2.cloned.1.call-start = ((), (), s32[]{:S(2)}) async-start(), calls=%async_computation.4 | async-start | bytes 4194304 | tf_op jit(solution)/shard_map/psum | solution.py:54
  276.4 190.9 %copy-start.5 = (s32[32]{0:T(128)S(1)}, s32[32]{0:T(128)}, u32[]{:S(2)}) copy-start(s32[32]{0:T(128)} %param.19) | copy-start | bytes 388
Sparse Core Ops, SparseCore 0:
  11.7 68.1 all-gather.4
  142.2 67.1 all-gather.6
  212.4 59.5 all-gather.10
  275.5 63.4 all-gather.8
  471.1 147.2 all-reduce.1
where the time goes:
time: 628 us
  blocking collectives  436 us (69%)
  waiting for transfers between devices  148 us (24%)
  matrix products  17.5 us (3%)
  between operations  14.1 us (2%)
  other arithmetic  6.33 us (1%)
    psum x3, blocking collectives, shards(): projection = lax.psum(partial_proj, 'tp')  373 us
    psum x1, waiting for transfers between devices, shards(): grad_total = lax.psum(partial_grad, 'pop')  147 us
    psum x1, blocking collectives, shards(): lax.psum(jnp.sum(readout_sum, axis=1), 'tp') / (episodes * step_count)  62.7 us
  transfers between devices with their start and end apart: 5, of which 1 were waited for; matrix products, arithmetic and copies ran while one was open for 2% of the time, Pallas kernels for 0%

commit v1 on v0

--- a/solution.py
+++ b/solution.py
@@ -51,7 +51,11 @@
     pre_side = jnp.take(full_table, pert_idx[:, 0], axis=0)
     weighted = pre_side.astype(jnp.float32) * fitness[:, None]
     partial_grad = jnp.dot(weighted.T, post_side, precision=lax.Precision.HIGHEST)
-    grad_total = lax.psum(partial_grad, "pop")
+    grad_total = partial_grad
+    for hop in (1, 2, 4, 8):
+        grad_total = grad_total + lax.ppermute(
+            grad_total, "pop", [(dev, dev ^ hop) for dev in range(16)]
+        )
     grad_rec = (grad_total * jnp.sqrt(12.0 / member_count)).astype(jnp.bfloat16)
     return (returns, grad_rec)
 

time: 628 us -> 1050 us (1.67)
  the two profiles are of different devices: /device:TPU:2 before, /device:TPU:1 now
where the time goes in v1:
time: 1050 us
  waiting for transfers between devices  453 us (43%)
  blocking collectives  441 us (42%)
  starting transfers between devices  118 us (11%)
  matrix products  15 us (1%)
  between operations  14.2 us (1%)
    ppermute x4, waiting for transfers between devices, shards(): lax.ppermute(grad_total, 'pop', [(dev, dev ^ hop) for dev in range(16)])  452 us
    psum x3, blocking collectives, shards(): projection = lax.psum(partial_proj, 'tp')  373 us
    ppermute x4, starting transfers between devices, shards(): lax.ppermute(grad_total, 'pop', [(dev, dev ^ hop) for dev in range(16)])  118 us
    psum x1, blocking collectives, shards(): lax.psum(jnp.sum(readout_sum, axis=1), 'tp') / (episodes * step_count)  67.7 us
  transfers between devices with their start and end apart: 8, of which 5 were waited for; matrix products, arithmetic and copies ran while one was open for 1% of the time, Pallas kernels for 0%

profile of v1, /device:TPU:1, one launch (start us, length us, event | category | flops | bytes accessed | tf_op | source)
XLA Modules:
  0.0 1053.0 jit_solution(747721626378910293)
XLA Ops:
  7.2 1.5 convert_element_type.59
  8.8 0.3 copy.12
  9.3 0.3 convolution_add_fusion
  9.7 0.7 divide_convert_fusion.5
  10.6 0.6 gather_fusion.2
  11.3 0.6 gather_fusion.1
  12.1 125.4 %psum.28 = f32[32,15]{1,0:T(8,128)S(1)} all-reduce(f32[32,15]{1,0:T(8,128)S(1)} %bitcast.55), channel_id=1, replica_groups=mesh['pop'=16,'tp'=32] {'tp'}, use_global_device_ids=true, to_apply=%region_0.0 | all-reduce | flops 480 | bytes 3840 | tf_op jit(solution)/shard_map/psum | solution.py:37
  137.8 4.0 divide_convert_fusion.4
  141.8 0.7 all-gather.11.cloned.1.call-update
  143.0 124.5 %psum.29 = f32[32,15]{1,0:T(8,128)S(1)} all-reduce(f32[32,15]{1,0:T(8,128)S(1)} %bitcast.56), channel_id=1, replica_groups=mesh['pop'=16,'tp'=32] {'tp'}, use_global_device_ids=true, to_apply=%region_1.3 | all-reduce | flops 480 | bytes 3840 | tf_op jit(solution)/shard_map/psum | solution.py:37
  267.6 4.0 divide_convert_fusion.3
  271.7 0.8 all-gather.11.cloned.1.call-done
  272.4 2.8 gather_fusion
  275.3 0.2 fusion.19
  275.7 0.3 divide_convert_fusion.1
  276.0 0.2 fusion.17
  276.4 0.2 fusion.21
  277.0 123.4 %psum.30 = f32[32,15]{1,0:T(8,128)S(1)} all-reduce(f32[32,15]{1,0:T(8,128)S(1)} %bitcast.54), channel_id=1, replica_groups=mesh['pop'=16,'tp'=32] {'tp'}, use_global_device_ids=true, to_apply=%region_2.4 | all-reduce | flops 480 | bytes 3840 | tf_op jit(solution)/shard_map/psum | solution.py:37
  400.4 3.3 fusion.42
  403.9 0.2 fusion.15
  404.4 67.7 %psum.31 = f32[32]{0:T(128)S(1)} all-reduce(f32[32]{0:T(128)S(1)} %fusion.30), channel_id=1, replica_groups=mesh['pop'=16,'tp'=32] {'tp'}, use_global_device_ids=true, to_apply=%region_4.6 | all-reduce | flops 32 | bytes 256 | tf_op jit(solution)/shard_map/psum | solution.py:48
  472.1 0.5 add_add_fusion.3
  472.6 1.9 fusion
  474.5 2.6 collective-permute-start
  477.1 45.8 %collective-permute-done = f32[4096,128]{1,0:T(8,128)S(1)} collective-permute-done((f32[4096,128]{1,0:T(8,128)S(1)}, f32[4096,128]{1,0:T(8,128)S(1)}, u32[]{:S(2)}, u32[]{:S(2)}) %collective-permute-start) | collective-permute-done | bytes 2097184 | tf_op jit(solution)/shard_map/ppermute | solution.py:56
  523.1 4.1 collective-permute-start.1
  527.2 90.3 %collective-permute-done.1 = f32[4096,128]{1,0:T(8,128)S(1)} collective-permute-done((f32[4096,128]{1,0:T(8,128)S(1)}, f32[4096,128]{1,0:T(8,128)S(1)}, u32[]{:S(2)}, u32[]{:S(2)}) %collective-permute-start.1) | collective-permute-done | bytes 2097184 | tf_op jit(solution)/shard_map/ppermute | solution.py:56
  617.7 8.1 collective-permute-start.2
  625.9 225.2 %collective-permute-done.2 = f32[4096,128]{1,0:T(8,128)S(1)} collective-permute-done((f32[4096,128]{1,0:T(8,128)S(1)}, f32[4096,128]{1,0:T(8,128)S(1)}, u32[]{:S(2)}, u32[]{:S(2)}) %collective-permute-start.2) | collective-permute-done | bytes 2097184 | tf_op jit(solution)/shard_map/ppermute | solution.py:56
  851.3 103.4 %collective-permute-start.3 = (f32[4096,128]{1,0:T(8,128)S(1)}, f32[4096,128]{1,0:T(8,128)S(1)}, u32[]{:S(2)}, u32[]{:S(2)}) collective-permute-start(f32[4096,128]{1,0:T(8,128)S(1)} %add.214), channel_id=1, source_target_pairs={{0,256},{32,288},{64,320},{96,352},{128,384},{160,416},{192,448},{... | collective-permute-start | bytes 6291464 | tf_op jit(solution)/shard_map/ppermute | solution.py:56
  954.6 90.6 %collective-permute-done.3 = f32[4096,128]{1,0:T(8,128)S(1)} collective-permute-done((f32[4096,128]{1,0:T(8,128)S(1)}, f32[4096,128]{1,0:T(8,128)S(1)}, u32[]{:S(2)}, u32[]{:S(2)}) %collective-permute-start.3) | collective-permute-done | bytes 2097184 | tf_op jit(solution)/shard_map/ppermute | solution.py:56
  1045.2 1.2 multiply_convert_fusion
  (66 shorter events, 3.3 us)
Async XLA Ops:
  7.2 130.6 %copy-start = (bf16[4096,128]{1,0:T(8,128)(2,1)S(1)}, bf16[4096,128]{1,0:T(8,128)(2,1)}, u32[]{:S(2)}) copy-start(bf16[4096,128]{1,0:T(8,128)(2,1)} %param.13) | copy-start | bytes 3145732
  7.2 2.1 copy-start.1
  7.2 2.1 copy-start.6
  7.2 130.6 %all-gather.5.cloned.1.call-start = ((), (), s32[]{:S(2)}) async-start(), calls=%async_computation | async-start | bytes 4055040 | tf_op jit(solution)/shard_map/all_gather | solution.py:30
  8.8 0.8 copy-start.4
  9.1 1.4 copy-start.5
  9.1 1.5 copy-start.2
  10.4 257.2 %all-gather.7.cloned.1.call-start = ((), (), s32[]{:S(2)}) async-start(), calls=%async_computation.1 | async-start | bytes 4055040 | tf_op jit(solution)/shard_map/all_gather | solution.py:30
  141.8 130.7 %all-gather.11.cloned.1.call-start = ((), (), s32[]{:S(2)}) async-start(), calls=%async_computation.3 | async-start | bytes 2162688 | tf_op jit(solution)/shard_map/all_gather | solution.py:50
  142.5 257.9 %all-gather.9.cloned.1.call-start = ((), (), s32[]{:S(2)}) async-start(), calls=%async_computation.2 | async-start | bytes 4055040 | tf_op jit(solution)/shard_map/all_gather | solution.py:30
  271.6 3.6 copy-start.3
  400.4 71.6 %copy-start.7 = (s32[32]{0:T(128)S(1)}, s32[32]{0:T(128)}, u32[]{:S(2)}) copy-start(s32[32]{0:T(128)} %param.19) | copy-start | bytes 388
  474.5 48.4 %collective-permute-start = (f32[4096,128]{1,0:T(8,128)S(1)}, f32[4096,128]{1,0:T(8,128)S(1)}, u32[]{:S(2)}, u32[]{:S(2)}) collective-permute-start(f32[4096,128]{1,0:T(8,128)S(1)} %fusion), channel_id=1, source_target_pairs={{0,32},{32,0},{64,96},{96,64},{128,160},{160,128},{192,224},{224,1... | collective-permute-start | bytes 6291464 | tf_op jit(solution)/shard_map/ppermute | solution.py:56
  523.1 94.4 %collective-permute-start.1 = (f32[4096,128]{1,0:T(8,128)S(1)}, f32[4096,128]{1,0:T(8,128)S(1)}, u32[]{:S(2)}, u32[]{:S(2)}) collective-permute-start(f32[4096,128]{1,0:T(8,128)S(1)} %add.212), channel_id=1, source_target_pairs={{0,64},{32,96},{64,0},{96,32},{128,192},{160,224},{192,128},{224,1... | collective-permute-start | bytes 6291464 | tf_op jit(solution)/shard_map/ppermute | solution.py:56
  617.7 233.3 %collective-permute-start.2 = (f32[4096,128]{1,0:T(8,128)S(1)}, f32[4096,128]{1,0:T(8,128)S(1)}, u32[]{:S(2)}, u32[]{:S(2)}) collective-permute-start(f32[4096,128]{1,0:T(8,128)S(1)} %add.213), channel_id=1, source_target_pairs={{0,128},{32,160},{64,192},{96,224},{128,0},{160,32},{192,64},{224,... | collective-permute-start | bytes 6291464 | tf_op jit(solution)/shard_map/ppermute | solution.py:56
  851.3 193.9 %collective-permute-start.3 = (f32[4096,128]{1,0:T(8,128)S(1)}, f32[4096,128]{1,0:T(8,128)S(1)}, u32[]{:S(2)}, u32[]{:S(2)}) collective-permute-start(f32[4096,128]{1,0:T(8,128)S(1)} %add.214), channel_id=1, source_target_pairs={{0,256},{32,288},{64,320},{96,352},{128,384},{160,416},{192,448},{... | collective-permute-start | bytes 6291464 | tf_op jit(solution)/shard_map/ppermute | solution.py:56
Sparse Core Ops, SparseCore 0:
  11.7 69.6 all-gather.4
  141.9 67.7 all-gather.6
  212.8 59.6 all-gather.10
  275.9 63.5 all-gather.8
